TPU v7x, 32 devices: a whole 2x2x4 slice. The times are simulated.
32 devices in a mesh: st: 8 (over y, x, core), fq: 4 (over z).
Axes of the slice: x: 2, y: 2, z: 4, core: 2. Of those that a mesh axis runs over, the one named last changes fastest.
Arguments:
- signals: bfloat16 [512, 16384], P(('st', 'fq')), may hold values from -6 to 6
- freq_bins: int32 [1024], replicated, may hold values from 1 to 8191, as said below
- sensor_station: int32 [512], P('st'), may hold values from 0 to 255, as said below
- gain: bfloat16 [512, 768], P('st'), may hold values from -1.5 to 1.5
- damping: float32 [256, 768], P('st'), may hold values from 0 to 1
- damping_up: float32 [256, 768], P('st'), may hold values from 0 to 1
- phase_speed: float32 [768], replicated, may hold values from 0.5 to 4
Outputs:
- estimate: bfloat16 [256, 768, 1024], P(('st', 'fq'))
Inputs may be any that keep to these rules, and one draw needn't show every extreme that they name: `freq_bins`: distinct bin numbers. `sensor_station`: sensor s sits at one of the 32 stations starting at (s // 64) * 32.
All inputs are finite; a program needn't handle non-finite values.
Results may differ from a plain program's by a relative error of at most 0.015.
Values may be sent and summed in bfloat16 or wider, within the bound.
A program may use at most 320 MiB of HBM per device.

v0:
```python
import math

import jax
import jax.numpy as jnp
from jax import lax
from jax.sharding import PartitionSpec as P

NT = 16384
NF = 1024
TOUT = 1024


def shifted(block, axis, distance):
    devices = range(lax.axis_size(axis))
    route = [(i - distance, i) for i in devices if i - distance in devices]
    return lax.ppermute(block, axis, route)


def cmul(left, right):
    return jnp.stack(
        [left[0] * right[0] - left[1] * right[1], left[0] * right[1] + left[1] * right[0]]
    )


def phases(steps, freq_bins):
    angle = (steps[:, None] * freq_bins[None, :] % NT).astype(jnp.float32) * (2 * math.pi / NT)
    return (jnp.cos(angle), jnp.sin(angle))


def base_table(count, freq_bins):
    fine = min(count, 128)
    coarse = count // fine
    fine_cos, fine_sin = phases(lax.iota(jnp.int32, fine), freq_bins)
    big_cos, big_sin = phases(lax.iota(jnp.int32, coarse) * fine, freq_bins)
    table_cos = big_cos[:, None, :] * fine_cos[None] - big_sin[:, None, :] * fine_sin[None]
    table_sin = big_sin[:, None, :] * fine_cos[None] + big_cos[:, None, :] * fine_sin[None]
    return (table_cos.reshape(count, -1), table_sin.reshape(count, -1))


def phase_rotated(base_cos, base_sine_table, offset, freq_bins):
    row_cos, row_sin = phases(jnp.reshape(offset, (1,)).astype(jnp.int32), freq_bins)
    return (
        base_cos * row_cos - base_sine_table * row_sin,
        base_sine_table * row_cos + base_cos * row_sin,
    )


def on_device(signals, freq_bins, sensor_station, gain, damping, damping_up, phase_speed):
    sens_dev = signals.shape[0]
    width = min(NT, 2048)
    base_cos, base_sine_table = base_table(width, freq_bins)

    def add_block(index, total):
        start = index * width
        times = start + lax.iota(jnp.int32, width)
        hann = 0.5 - 0.5 * jnp.cos(times.astype(jnp.float32) * (2 * math.pi / NT))
        piece = lax.dynamic_slice_in_dim(signals, start, width, 1)
        windowed = (piece.astype(jnp.float32) * hann[None, :]).astype(jnp.bfloat16)
        turned_cos, shifted_imaginary_factor = phase_rotated(
            base_cos, base_sine_table, start, freq_bins
        )
        table = jnp.concatenate(
            [
                (turned_cos / math.sqrt(NT)).astype(jnp.bfloat16),
                (shifted_imaginary_factor / math.sqrt(NT)).astype(jnp.bfloat16),
            ],
            axis=1,
        )
        return total + jnp.dot(windowed, table, preferred_element_type=jnp.float32)

    spectra = lax.fori_loop(0, NT // width, add_block, jnp.zeros((sens_dev, 2 * NF), jnp.float32))
    spec_re = spectra[:, :NF].astype(jnp.bfloat16)
    spec_im = (-spectra[:, NF:]).astype(jnp.bfloat16)
    spec_re, spec_im = (
        lax.all_to_all(spec_re, "fq", split_axis=1, concat_axis=0, tiled=True),
        lax.all_to_all(spec_im, "fq", split_axis=1, concat_axis=0, tiled=True),
    )
    sens_block = spec_re.shape[0]
    freq_dev = spec_re.shape[1]
    width_state = gain.shape[1]
    st_dev = damping.shape[0]
    own_bins = lax.dynamic_slice_in_dim(freq_bins, lax.axis_index("fq") * freq_dev, freq_dev)
    theta = 2 * math.pi * (own_bins.astype(jnp.float32) / NT)[:, None] * phase_speed[None, :]
    rot_down = jnp.stack([jnp.cos(theta), -jnp.sin(theta)])
    rot_up = jnp.stack([jnp.cos(theta), jnp.sin(theta)])
    local = sensor_station - lax.axis_index("st") * st_dev
    onehot = (local[None, :] == lax.iota(jnp.int32, st_dev)[:, None]).astype(jnp.bfloat16)
    spec_own = jnp.stack([spec_re, spec_im]).transpose(0, 2, 1)
    selected = onehot[:, None, None, :] * spec_own[None]
    forcing = jnp.dot(selected.reshape(-1, sens_block), gain, preferred_element_type=jnp.float32)
    forcing = forcing.reshape(st_dev, 2, freq_dev, width_state)
    zeros = jnp.zeros((2, freq_dev, width_state), jnp.float32)
    identity = jnp.stack(
        [
            jnp.ones((freq_dev, width_state), jnp.float32),
            jnp.zeros((freq_dev, width_state), jnp.float32),
        ]
    )

    def march_down(carry, inputs):
        state, product = carry
        term, rate = inputs
        factor = rate[None, None, :] * rot_down
        state = cmul(factor, state) + term
        return ((state, cmul(factor, product)), state)

    (last_down, block_down), downstream_fields = lax.scan(
        march_down, (zeros, identity), (forcing, damping)
    )

    def march_upward(carry, inputs):
        state, product = carry
        term, rate, lower = inputs
        factor = rate[None, None, :] * rot_up
        state = cmul(factor, state) + term
        return ((state, cmul(factor, product)), state + lower)

    (first_up, block_up), partial_sum = lax.scan(
        march_upward, (zeros, identity), (forcing, damping_up, downstream_fields), reverse=True
    )

    def relay(turn, carry):
        from_below, from_above = carry
        output_downward = cmul(block_down, from_below) + last_down
        out_up = cmul(block_up, from_above) + first_up
        from_below = shifted(output_downward.astype(jnp.bfloat16), "st", 1).astype(
            output_downward.dtype
        )
        from_above = shifted(out_up.astype(jnp.bfloat16), "st", -1).astype(out_up.dtype)
        return (from_below, from_above)

    from_below, from_above = lax.fori_loop(0, lax.axis_size("st") - 1, relay, (zeros, zeros))

    def carry_down(state, rate):
        state = cmul(rate[None, None, :] * rot_down, state)
        return (state, state)

    ending_down, lifted_down = lax.scan(carry_down, from_below, damping)

    def carry_up(state, inputs):
        rate, base, lower = inputs
        state = cmul(rate[None, None, :] * rot_up, state)
        return (state, (base + lower + state).astype(jnp.bfloat16))

    ending_up, state_all = lax.scan(
        carry_up, from_above, (damping_up, partial_sum, lifted_down), reverse=True
    )
    out_cos, out_sin = base_table(TOUT, freq_bins)
    out_cos, out_sin = phase_rotated(out_cos, out_sin, NT - TOUT, freq_bins)
    inverse = jnp.stack(
        [
            (out_cos.T / math.sqrt(NF)).astype(jnp.bfloat16),
            (-out_sin.T / math.sqrt(NF)).astype(jnp.bfloat16),
        ]
    )
    return jnp.einsum(
        "kcfm,cft->kmt",
        lax.all_to_all(state_all, "fq", split_axis=0, concat_axis=2, tiled=True),
        inverse,
        preferred_element_type=jnp.float32,
    ).astype(jnp.bfloat16)


def solution(mesh):
    placed = (P(("st", "fq"), None), P(), P("st"), P("st", None), P("st", None), P("st", None), P())
    return jax.shard_map(
        on_device,
        mesh=mesh,
        in_specs=placed,
        out_specs=P(("st", "fq"), None, None),
        check_vma=False,
    )
```

profile of v0, /device:TPU:4, one launch (start us, length us, event | category | flops | bytes accessed | tf_op | source)
XLA Modules:
  0.0 2022.5 jit_solution(1297842721965463363)
XLA Ops:
  3.8 110.0 %while.98 = (s32[]{:T(128)}, f32[16,2048]{1,0:T(8,128)S(1)}, bf16[16,16384]{1,0:T(8,128)(2,1)}, s32[1024]{0:T(1024)}, f32[128,1024]{1,0:T(8,128)S(1)}, /*index=5...) while((s32[]{:T(128)}, f32[16,2048]{1,0:T(8,128)S(1)}, ...), condition=%wide.region_1.2_spmd.clone.clone.clone, body=%wide.region_0.1_spmd.clone.clone.clone.sunk | while | flops 184737792 | bytes 51876020 | solution.py:71
  7.0 5.8 fusion.92
  20.7 5.8 fusion.92
  34.5 5.8 fusion.92
  48.2 5.8 fusion.92
  62.0 5.8 fusion.92
  75.7 5.8 fusion.92
  89.5 5.8 fusion.92
  103.2 5.8 fusion.92
  114.5 4.9 all-to-all-start
  135.5 20.2 fusion.44
  155.7 16.3 broadcast.585.clone
  173.3 316.1 %while.95 = (s32[]{:T(128)}, f32[2,256,768]{2,1,0:T(8,128)}, f32[2,256,768]{2,1,0:T(8,128)}, f32[32,2,256,768]{3,2,1,0:T(8,128)}, f32[32,768]{1,0:T(8,128)}, /*i...) while((s32[]{:T(128)}, f32[2,256,768]{2,1,0:T(8,128)}, ...), condition=%wide.region_3.4_spmd.clone, body=%wide.region_2.3_spmd.clone.sunk | while | flops 5111811 | bytes 33040012 | solution.py:107
  489.4 16.2 broadcast.585.clone.1
  507.0 333.9 %while.96 = (s32[]{:T(128)}, f32[2,256,768]{2,1,0:T(8,128)}, f32[2,256,768]{2,1,0:T(8,128)}, f32[32,2,256,768]{3,2,1,0:T(8,128)}, f32[32,768]{1,0:T(8,128)}, /*i...) while((s32[]{:T(128)}, f32[2,256,768]{2,1,0:T(8,128)}, ...), condition=%wide.region_5.6_spmd.clone, body=%wide.region_4.5_spmd.clone.sunk | while | flops 5505028 | bytes 34612392 | solution.py:118
  841.0 217.8 %while.97 = (s32[]{:T(128)}, f32[2,256,768]{2,1,0:T(8,128)}, f32[2,256,768]{2,1,0:T(8,128)}, f32[2,256,768]{2,1,0:T(8,128)}, f32[2,256,768]{2,1,0:T(8,128)}, /*i...) while((s32[]{:T(128)}, f32[2,256,768]{2,1,0:T(8,128)}, ...), condition=%wide.region_7.8_spmd.clone, body=%wide.region_6.7_spmd.clone.sunk | while | flops 6291459 | bytes 66060612 | solution.py:132
  852.1 10.8 collective-permute-done.1
  882.8 11.7 collective-permute-done.1
  913.2 12.5 collective-permute-done.1
  944.5 12.8 collective-permute-done.1
  976.1 13.1 collective-permute-done.1
  1008.0 13.5 collective-permute-done.1
  1040.2 13.8 collective-permute-done.1
  1058.8 16.2 broadcast.585
  1075.0 137.9 %while.93 = (s32[]{:T(128)}, f32[2,256,768]{2,1,0:T(8,128)}, f32[32,2,256,768]{3,2,1,0:T(8,128)}, f32[32,768]{1,0:T(8,128)}, f32[2,256,768]{2,1,0:T(8,128)S(1)}, /*index=5*/s32[]{:T(128)}) while((s32[]{:T(128)}, f32[2,256,768]{2,1,0:T(8,128)}, f32[32,2,256,768]{3,2,1,0:T(8,128)}, f32[32,768]{1,0:T(8,128)}, f32[2,256,768]{2,1,0:T(8,128)S(1)}, ...), condition=%wide.region_9.10_spmd, body=%wide.region_8.9_spmd.sunk | while | flops 1966082 | bytes 18884196 | solution.py:138
  1212.9 8.8 broadcast_in_dim.20
  1221.7 138.6 %while.94 = (s32[]{:T(128)}, f32[2,256,768]{2,1,0:T(8,128)S(1)}, bf16[32,2,256,768]{3,2,1,0:T(8,128)(2,1)}, f32[32,768]{1,0:T(8,128)}, f32[2,256,768]{2,1,0:T(8,...) while((s32[]{:T(128)}, f32[2,256,768]{2,1,0:T(8,128)S(1)}, ...), condition=%wide.region_11.12_spmd, body=%wide.region_10.11_spmd.sunk | while | flops 3538947 | bytes 16524401 | solution.py:145
  1360.3 8.8 all-to-all-start.2
  1375.8 535.3 %all-to-all-done.2 = bf16[32,2,256,768]{3,2,1,0:T(8,128)(2,1)} async-done(((bf16[32,2,256,768]{3,2,1,0:T(8,128)(2,1)}), bf16[32,2,256,768]{3,2,1,0:T(8,128)(2,1)}, u32[]{:S(2)}, u32[]{:S(2)}) %all-to-all-start.2) | async-done | bytes 25165856 | tf_op jit(solution)/shard_map/all_to_all | solution.py:158
  1911.1 38.9 %copy.26 = bf16[4,8,2,256,768]{3,0,4,2,1:T(4,128)(2,1)} copy(bf16[4,8,2,256,768]{4,3,2,1,0:T(8,128)(2,1)} %bitcast.10) | data formatting | bytes 50331648 | tf_op jit(solution)/shard_map/all_to_all | solution.py:158
  1949.9 40.6 %all_to_all.46 = bf16[8,2,1024,768]{2,3,1,0:T(8,128)(2,1)} reshape(bf16[8,2,4,256,768]{3,2,4,1,0:T(4,128)(2,1)} %bitcast.140) | data formatting | bytes 50331648 | tf_op jit(solution)/shard_map/all_to_all | solution.py:158
  1990.5 32.0 %bitcast_convert_fusion = bf16[8,768,1024]{2,1,0:T(8,128)(2,1)} fusion(bf16[8,2,1024,768]{2,3,1,0:T(8,128)(2,1)} %all_to_all.46, bf16[1,1024,1024]{2,1,0:T(8,128)(2,1)} %get-tuple-element.875, bf16[1,1024,1024]{2,1,0:T(8,128)(2,1)S(1)} %get-tuple-element.874), kind=kOutput, calls=%fused_computation.80 | convolution fusion | flops 25778192384 | bytes 41943040 | tf_op jit(solution)/shard_map/kcfm,cft->kmt/dot_general | solution.py:156
  (1090 shorter events, 1145.0 us)
Async XLA Ops:
  0.0 135.5 %copy-start = (bf16[64,768]{1,0:T(8,128)(2,1)S(1)}, bf16[64,768]{1,0:T(8,128)(2,1)}, u32[]{:S(2)}) copy-start(bf16[64,768]{1,0:T(8,128)(2,1)} %param.22) | copy-start | bytes 294916
  3.8 116.3 %copy-start.16 = (f32[768]{0:T(1024)S(1)}, f32[768]{0:T(1024)}, u32[]{:S(2)}) copy-start(f32[768]{0:T(1024)} %param.25) | copy-start | bytes 9220
  113.8 16.0 copy-start.11
  113.8 16.0 copy-start.13
  113.8 10.3 copy-start.18
  114.5 10.5 all-to-all-start
  125.0 10.5 all-to-all-start.1
  155.7 16.3 copy-start.17
  846.7 16.2 collective-permute-start.1
  849.7 19.0 collective-permute-start
  877.3 17.1 collective-permute-start.1
  880.4 17.5 collective-permute-start
  905.5 4.8 copy-start.10
  906.5 19.2 collective-permute-start.1
  911.3 16.9 collective-permute-start
  935.7 5.8 copy-start.10
  936.8 20.6 %collective-permute-start.1 = (bf16[2,256,768]{2,1,0:T(8,128)(2,1)}, bf16[2,256,768]{2,1,0:T(8,128)(2,1)}, u32[]{:S(2)}, u32[]{:S(2)}) collective-permute-start(bf16[2,256,768]{2,1,0:T(8,128)(2,1)} %fusion.89), channel_id=1, source_target_pairs={{4,0},{8,4},{12,8},{16,12},{20,16},{24,20},{28,24},{5,1},{9,5},{13... | collective-permute-start | bytes 2359304 | tf_op jit(solution)/shard_map/while/body/eval_jaxpr/ppermute | solution.py:16
  942.6 17.2 collective-permute-start
  967.3 5.8 copy-start.10
  968.4 20.9 %collective-permute-start.1 = (bf16[2,256,768]{2,1,0:T(8,128)(2,1)}, bf16[2,256,768]{2,1,0:T(8,128)(2,1)}, u32[]{:S(2)}, u32[]{:S(2)}) collective-permute-start(bf16[2,256,768]{2,1,0:T(8,128)(2,1)} %fusion.89), channel_id=1, source_target_pairs={{4,0},{8,4},{12,8},{16,12},{20,16},{24,20},{28,24},{5,1},{9,5},{13... | collective-permute-start | bytes 2359304 | tf_op jit(solution)/shard_map/while/body/eval_jaxpr/ppermute | solution.py:16
  974.2 17.5 collective-permute-start
  999.2 5.8 copy-start.10
  1000.3 21.2 %collective-permute-start.1 = (bf16[2,256,768]{2,1,0:T(8,128)(2,1)}, bf16[2,256,768]{2,1,0:T(8,128)(2,1)}, u32[]{:S(2)}, u32[]{:S(2)}) collective-permute-start(bf16[2,256,768]{2,1,0:T(8,128)(2,1)} %fusion.89), channel_id=1, source_target_pairs={{4,0},{8,4},{12,8},{16,12},{20,16},{24,20},{28,24},{5,1},{9,5},{13... | collective-permute-start | bytes 2359304 | tf_op jit(solution)/shard_map/while/body/eval_jaxpr/ppermute | solution.py:16
  1006.1 17.8 collective-permute-start
  1031.4 5.8 copy-start.10
  1032.5 21.5 %collective-permute-start.1 = (bf16[2,256,768]{2,1,0:T(8,128)(2,1)}, bf16[2,256,768]{2,1,0:T(8,128)(2,1)}, u32[]{:S(2)}, u32[]{:S(2)}) collective-permute-start(bf16[2,256,768]{2,1,0:T(8,128)(2,1)} %fusion.89), channel_id=1, source_target_pairs={{4,0},{8,4},{12,8},{16,12},{20,16},{24,20},{28,24},{5,1},{9,5},{13... | collective-permute-start | bytes 2359304 | tf_op jit(solution)/shard_map/while/body/eval_jaxpr/ppermute | solution.py:16
  1038.3 18.1 collective-permute-start
  1212.9 8.8 copy-start.8
  1360.3 8.8 copy-start.14
  1360.3 9.0 copy-start.12
  1360.3 550.7 %all-to-all-start.2 = ((bf16[32,2,256,768]{3,2,1,0:T(8,128)(2,1)}), bf16[32,2,256,768]{3,2,1,0:T(8,128)(2,1)}, u32[]{:S(2)}, u32[]{:S(2)}) async-start(bf16[32,2,256,768]{3,2,1,0:T(8,128)(2,1)} %get-tuple-element.577), calls=%async_computation.2 | async-start | bytes 50331648 | tf_op jit(solution)/shard_map/all_to_all | solution.py:158
  1990.5 32.0 %copy-start.1 = (bf16[64,768]{1,0:T(8,128)(2,1)S(1)}, bf16[64,768]{1,0:T(8,128)(2,1)}, u32[]{:S(2)}) copy-start(bf16[64,768]{1,0:T(8,128)(2,1)} %param.22) | copy-start | bytes 294916
  (127 other events, 216.8 us)
where the time goes:
time: 2040 us; the launch traced here: 2020 us
  other arithmetic  925 us (45%)
  waiting for transfers between devices  632 us (31%)
  local copies, waits for them, and re-layouts  312 us (15%)
  matrix products  89.8 us (4%)
  starting transfers between devices  59.2 us (3%)
    all_to_all x1, waiting for transfers between devices, on_device(): lax.all_to_all(state_all, 'fq', split_axis=0, concat_axis=2, tiled=True)  535 us
    dynamic_update_slice x96, other arithmetic, on_device(): lax.scan(march_down, (zeros, identity), (forcing, damping))  259 us
    while x78, other arithmetic  119 us
    dynamic_update_slice x32, other arithmetic, on_device(): lax.scan(carry_up, from_above, (damping_up, partial_sum, lifted_down), re...  100 us
    dynamic_slice x128, local copies, waits for them, and re-layouts, on_device(): lax.scan(march_down, (zeros, identity), (forcing, damping))  96.4 us
    ppermute x14, waiting for transfers between devices, shifted(): return lax.ppermute(block, axis, route)  92.6 us
    add x32, other arithmetic, march_upward(): state = cmul(factor, state) + term  89.2 us
    add x32, other arithmetic, march_down(): state = cmul(factor, state) + term  88.3 us
  transfers between devices with their start and end apart: 17, of which 12 were waited for; matrix products, arithmetic and copies ran while one was open for 2% of the time, Pallas kernels for 0%

commit v1 on v0

v1 whole, which is shorter than its diff:
```python
import functools
import math

import jax
import jax.numpy as jnp
from jax import lax
from jax.experimental import pallas as pl
from jax.experimental.pallas import tpu as pltpu
from jax.sharding import PartitionSpec as P

NT = 16384
NF = 1024
TOUT = 1024
CHUNKS = 3
TILE = 128
SUB = 16
F32 = jnp.float32
BF16 = jnp.bfloat16


def shifted(block, axis, distance):
    devices = range(lax.axis_size(axis))
    route = [(i - distance, i) for i in devices if i - distance in devices]
    return lax.ppermute(block, axis, route)


def cmul(left, right):
    return (left[0] * right[0] - left[1] * right[1], left[0] * right[1] + left[1] * right[0])


def cpow(base, n):
    out = None
    while n:
        if n & 1:
            out = base if out is None else cmul(out, base)
        n >>= 1
        if n:
            base = cmul(base, base)
    return out


def angles(left, right):
    return (left * right % NT).astype(F32) * (2 * math.pi / NT)


def spectrum_kernel(x_ref, lc_ref, ls_ref, hc_ref, hs_ref, out_ref):
    hc, hs = hc_ref[...], hs_ref[...]
    re, im = [], []
    for s in range(x_ref.shape[0]):
        a = jnp.dot(x_ref[s], lc_ref[...], preferred_element_type=F32)
        b = jnp.dot(x_ref[s], ls_ref[...], preferred_element_type=F32)
        re.append(jnp.sum(hc * a - hs * b, axis=0, keepdims=True))
        im.append(-jnp.sum(hs * a + hc * b, axis=0, keepdims=True))
    scale = 1.0 / math.sqrt(NT)
    out_ref[0] = (jnp.concatenate(re, axis=0) * scale).astype(BF16)
    out_ref[1] = (jnp.concatenate(im, axis=0) * scale).astype(BF16)


def spectrum(signals, freq_bins):
    sens = signals.shape[0]
    fine = 128
    coarse = NT // fine
    times = lax.iota(jnp.int32, NT)
    hann = 0.5 - 0.5 * jnp.cos(times.astype(F32) * (2 * math.pi / NT))
    windowed = (signals.astype(F32) * hann[None, :]).astype(BF16).reshape(sens, coarse, fine)
    low = angles(lax.iota(jnp.int32, fine)[:, None], freq_bins[None, :])
    high = angles(lax.iota(jnp.int32, coarse)[:, None] * fine, freq_bins[None, :])
    ft = 256
    table = pl.BlockSpec((fine, ft), lambda i: (0, i))
    big = pl.BlockSpec((coarse, ft), lambda i: (0, i))
    return pl.pallas_call(
        spectrum_kernel,
        grid=(NF // ft,),
        in_specs=[pl.BlockSpec((sens, coarse, fine), lambda i: (0, 0, 0)), table, table, big, big],
        out_specs=pl.BlockSpec((2, sens, ft), lambda i: (0, 0, i)),
        out_shape=jax.ShapeDtypeStruct((2, sens, NF), BF16),
        cost_estimate=pl.CostEstimate(
            flops=4 * sens * NT * NF, bytes_accessed=4 << 20, transcendentals=0
        ),
        name="spectrum",
    )(windowed, jnp.cos(low).astype(BF16), jnp.sin(low).astype(BF16), jnp.cos(high), jnp.sin(high))


def step_down(state, rate, c, s, fr, fi):
    re, im = state
    return (rate * (re * c + im * s) + fr, rate * (im * c - re * s) + fi)


def step_up(state, rate, c, s, fr, fi):
    re, im = state
    return (rate * (re * c - im * s) + fr, rate * (im * c + re * s) + fi)


def ends_kernel(own, mg_ref, spec_ref, c_ref, s_ref, dd_ref, du_ref, down_ref, up_ref, f_ref):
    count, tile, sens = mg_ref.shape
    fd = c_ref.shape[1]

    def sub(i, unused):
        rows = pl.ds(pl.multiple_of(i * SUB, SUB), SUB)
        left = mg_ref[:, rows, :].reshape(count * SUB, sens)
        f_ref[...] = jnp.dot(left, spec_ref[...], preferred_element_type=F32).reshape(
            count, SUB, 2 * fd
        )
        c, s = c_ref[rows, :], s_ref[rows, :]
        rd, ru = dd_ref[rows, :], du_ref[rows, :]
        down = up = (jnp.zeros((SUB, fd), F32), jnp.zeros((SUB, fd), F32))
        for k in range(count):
            down = step_down(down, rd[:, k : k + 1], c, s, f_ref[k, :, :fd], f_ref[k, :, fd:])
            b = count - 1 - k
            up = step_up(up, ru[:, b : b + 1], c, s, f_ref[b, :, :fd], f_ref[b, :, fd:])
            if (k + 1) % own == 0:
                q = (k + 1) // own - 1
                down_ref[q, 0, rows, :], down_ref[q, 1, rows, :] = down
                up_ref[q, 0, rows, :], up_ref[q, 1, rows, :] = up
        return unused

    lax.fori_loop(0, tile // SUB, sub, 0)


def block_ends(own, mg, spec, c, s, dd, du):
    count, width, sens = mg.shape
    fd = c.shape[1]
    parts = count // own
    tiles = width // TILE
    row = lambda i: (i, 0)
    out = jax.ShapeDtypeStruct((parts, 2, tiles * TILE, fd), F32)
    out_spec = pl.BlockSpec((parts, 2, TILE, fd), lambda i: (0, 0, i, 0))
    return pl.pallas_call(
        functools.partial(ends_kernel, own),
        grid=(tiles,),
        in_specs=[
            pl.BlockSpec((count, TILE, sens), lambda i: (0, i, 0)),
            pl.BlockSpec((sens, 2 * fd), lambda i: (0, 0)),
            pl.BlockSpec((TILE, fd), row),
            pl.BlockSpec((TILE, fd), row),
            pl.BlockSpec((TILE, count), row),
            pl.BlockSpec((TILE, count), row),
        ],
        out_specs=[out_spec, out_spec],
        out_shape=[out, out],
        scratch_shapes=[pltpu.VMEM((count, SUB, 2 * fd), F32)],
        cost_estimate=pl.CostEstimate(
            flops=8 * 256 * count * tiles * TILE * fd, bytes_accessed=8 << 20, transcendentals=0
        ),
        name="block_ends",
    )(mg, spec, c, s, dd, du)


def march_kernel(mg_ref, spec_ref, c_ref, s_ref, dd_ref, du_ref, in_ref, inv_ref, *rest):
    out_ref, f_ref, d_ref, state_ref = rest[-4:]
    own, tile, sens = mg_ref.shape
    parts, _, _, fd = in_ref.shape

    def sub(i, unused):
        rows = pl.ds(pl.multiple_of(i * SUB, SUB), SUB)
        left = mg_ref[:, rows, :].reshape(own * SUB, sens)
        f_ref[...] = jnp.dot(left, spec_ref[...], preferred_element_type=F32).reshape(
            own, SUB, 2 * NF
        )
        rd, ru = dd_ref[rows, :], du_ref[rows, :]
        for j in range(parts):
            lo, hi = slice(j * fd, (j + 1) * fd), slice(NF + j * fd, NF + (j + 1) * fd)
            c, s = c_ref[rows, lo], s_ref[rows, lo]
            down = (in_ref[j, 0, rows, :].astype(F32), in_ref[j, 1, rows, :].astype(F32))
            for k in range(own):
                down = step_down(down, rd[:, k : k + 1], c, s, f_ref[k, :, lo], f_ref[k, :, hi])
                d_ref[k, 0], d_ref[k, 1] = down
            up = (in_ref[j, 2, rows, :].astype(F32), in_ref[j, 3, rows, :].astype(F32))
            for k in reversed(range(own)):
                up = step_up(up, ru[:, k : k + 1], c, s, f_ref[k, :, lo], f_ref[k, :, hi])
                state_ref[k, rows, lo] = (d_ref[k, 0] + up[0]).astype(BF16)
                state_ref[k, rows, hi] = (d_ref[k, 1] + up[1]).astype(BF16)
        return unused

    lax.fori_loop(0, tile // SUB, sub, 0)
    step = 256

    def columns(n, unused):
        cols = pl.ds(pl.multiple_of(n * step, step), step)
        got = jnp.dot(
            state_ref[...].reshape(own * tile, 2 * NF),
            inv_ref[:, cols],
            preferred_element_type=F32,
        )
        out_ref[:, :, cols] = got.reshape(own, tile, step).astype(BF16)
        return unused

    lax.fori_loop(0, TOUT // step, columns, 0)


def estimate_chunk(chunk, mg, spec, c, s, dd, du, entering, inverse, filled):
    own, width, sens = mg.shape
    parts, _, wide, fd = entering.shape
    tiles = wide // TILE
    row = lambda i: (chunk * tiles + i, 0)
    specs = [
        pl.BlockSpec((own, TILE, sens), lambda i: (0, chunk * tiles + i, 0)),
        pl.BlockSpec((sens, 2 * NF), lambda i: (0, 0)),
        pl.BlockSpec((TILE, NF), row),
        pl.BlockSpec((TILE, NF), row),
        pl.BlockSpec((TILE, own), row),
        pl.BlockSpec((TILE, own), row),
        pl.BlockSpec((parts, 4, TILE, fd), lambda i: (0, 0, i, 0)),
        pl.BlockSpec((2 * NF, TOUT), lambda i: (0, 0)),
    ]
    args = [mg, spec, c, s, dd, du, entering, inverse]
    aliases = {}
    if filled is not None:
        aliases = {len(args): 0}
        specs.append(pl.BlockSpec(memory_space=pl.ANY))
        args.append(filled)
    return pl.pallas_call(
        march_kernel,
        grid=(tiles,),
        in_specs=specs,
        out_specs=pl.BlockSpec((own, TILE, TOUT), lambda i: (0, chunk * tiles + i, 0)),
        out_shape=jax.ShapeDtypeStruct((own, width, TOUT), BF16),
        scratch_shapes=[
            pltpu.VMEM((own, SUB, 2 * NF), F32),
            pltpu.VMEM((own, 2, SUB, fd), F32),
            pltpu.VMEM((own, TILE, 2 * NF), BF16),
        ],
        input_output_aliases=aliases,
        cost_estimate=pl.CostEstimate(
            flops=12 * own * wide * NF * TOUT, bytes_accessed=16 << 20, transcendentals=0
        ),
        name="march",
    )(*args)


def masked_gain(local, first, count, gain_t):
    stations = first + lax.iota(jnp.int32, count)
    hit = local[None, None, :] == stations[:, None, None]
    return jnp.where(hit, gain_t[None], jnp.zeros((), BF16))


def rotation(freq_bins, phase_speed):
    turn = 2 * math.pi * (freq_bins.astype(F32) / NT)
    theta = phase_speed[:, None] * turn[None, :]
    return jnp.cos(theta), jnp.sin(theta)


def inverse_table(freq_bins):
    fine = 128
    low = angles(freq_bins[:, None], lax.iota(jnp.int32, fine)[None, :])
    steps = NT - TOUT + fine * lax.iota(jnp.int32, TOUT // fine)
    high = angles(freq_bins[:, None], steps[None, :])
    lc, ls, hc, hs = lax.optimization_barrier(
        (jnp.cos(low), jnp.sin(low), jnp.cos(high), jnp.sin(high))
    )
    scale = 1.0 / math.sqrt(NF)
    hc, hs = hc * scale, hs * scale
    cosines, sines = [], []
    for h in range(TOUT // fine):
        a, b = hc[:, h : h + 1], hs[:, h : h + 1]
        cosines.append((a * lc - b * ls).astype(BF16))
        sines.append((-(b * lc + a * ls)).astype(BF16))
    return jnp.concatenate(
        [jnp.concatenate(cosines, axis=1), jnp.concatenate(sines, axis=1)], axis=0
    )


def on_device(signals, freq_bins, sensor_station, gain, damping, damping_up, phase_speed):
    parts = lax.axis_size("fq")
    mine = lax.axis_index("fq")
    st_dev, width = damping.shape
    own = st_dev // parts
    fd = NF // parts
    sens = gain.shape[0]

    spec = spectrum(signals, freq_bins)
    spec = lax.all_to_all(
        jnp.broadcast_to(spec[None], (parts,) + spec.shape), "fq", 0, 0, tiled=True
    )
    spec = spec.transpose(0, 2, 1, 3).reshape(sens, 2, NF)
    spec_own = lax.dynamic_slice_in_dim(spec, mine * fd, fd, 2).reshape(sens, 2 * fd)
    spec = spec.reshape(sens, 2 * NF)

    own_bins = lax.dynamic_slice_in_dim(freq_bins, mine * fd, fd)
    c, s = rotation(own_bins, phase_speed)
    local = sensor_station - lax.axis_index("st") * st_dev
    gain_t = gain.T
    mg = masked_gain(local, 0, st_dev, gain_t)
    dd, du = damping.T, damping_up.T
    chunk_width = width // CHUNKS

    c_all, s_all = rotation(freq_bins, phase_speed)
    mg_own = masked_gain(local, mine * own, own, gain_t)
    dd_own = lax.dynamic_slice_in_dim(dd, mine * own, own, 1)
    du_own = lax.dynamic_slice_in_dim(du, mine * own, own, 1)
    inverse = inverse_table(freq_bins)

    down_loc, up_loc = block_ends(own, mg, spec_own, c, s, dd, du)
    unit = cpow((c, s), own)
    turns = [unit]
    for j in range(1, parts):
        turns.append(cmul(turns[-1], unit))
    turns = lax.optimization_barrier(turns)

    def down_factor(j):
        rate = jnp.prod(damping[: j * own], axis=0)[:, None]
        return (rate * turns[j - 1][0], -rate * turns[j - 1][1])

    def up_factor(j):
        rate = jnp.prod(damping_up[st_dev - j * own :], axis=0)[:, None]
        return (rate * turns[j - 1][0], rate * turns[j - 1][1])

    full_down, full_up = lax.optimization_barrier((down_factor(parts), up_factor(parts)))
    below = above = jnp.zeros((2, width, fd), F32)
    for hop in range(lax.axis_size("st") - 1):
        out_down = jnp.stack(cmul(full_down, below)) + down_loc[parts - 1]
        out_up = jnp.stack(cmul(full_up, above)) + up_loc[parts - 1]
        below = shifted(out_down.astype(BF16), "st", 1).astype(F32)
        above = shifted(out_up.astype(BF16), "st", -1).astype(F32)
    entering = []
    for i in range(CHUNKS):
        rows = slice(i * chunk_width, (i + 1) * chunk_width)
        pieces = []
        for q in range(parts):
            down_in, up_in = below[:, rows], above[:, rows]
            if q > 0:
                down_in = (jnp.stack(cmul(down_factor(q), below)) + down_loc[q - 1])[:, rows]
            if q < parts - 1:
                lifted = jnp.stack(cmul(up_factor(parts - 1 - q), above))
                up_in = (lifted + up_loc[parts - 2 - q])[:, rows]
            pieces.append(jnp.concatenate([down_in, up_in], axis=0).astype(BF16))
        entering.append(lax.all_to_all(jnp.stack(pieces), "fq", 0, 0, tiled=True))

    result = None
    for i in range(CHUNKS):
        result = estimate_chunk(
            i, mg_own, spec, c_all, s_all, dd_own, du_own, entering[i], inverse, result
        )
    return result


def solution(mesh):
    placed = (P(("st", "fq"), None), P(), P("st"), P("st", None), P("st", None), P("st", None), P())
    return jax.shard_map(
        on_device,
        mesh=mesh,
        in_specs=placed,
        out_specs=P(("st", "fq"), None, None),
        check_vma=False,
    )
```

time: 2040 us -> 416 us (0.20)
  the two profiles are of different devices: /device:TPU:4 before, /device:TPU:10 now
where the time goes in v1:
time: 416 us; the launch traced here: 415 us
  starting transfers between devices  141 us (34%)
  Pallas kernels  106 us (25%)
  waiting for transfers between devices  82.5 us (20%)
  other arithmetic  66.2 us (16%)
  local copies, waits for them, and re-layouts  18.4 us (4%)
    ppermute x14, starting transfers between devices, shifted(): return lax.ppermute(block, axis, route)  116 us
    pallas_call x3, Pallas kernels, estimate_chunk(): pl.pallas_call(march_kernel, grid=(tiles,), in_specs=specs, out_specs=pl....  73.5 us
    all_to_all x3, waiting for transfers between devices, on_device(): entering.append(lax.all_to_all(jnp.stack(pieces), 'fq', 0, 0, tiled=True))  55.8 us
    pallas_call x1, Pallas kernels, block_ends(): pl.pallas_call(functools.partial(ends_kernel, own), grid=(tiles,), in_spe...  26.9 us
    ppermute x14, waiting for transfers between devices, shifted(): return lax.ppermute(block, axis, route)  26.8 us
    all_to_all x3, starting transfers between devices, on_device(): entering.append(lax.all_to_all(jnp.stack(pieces), 'fq', 0, 0, tiled=True))  19.7 us
    sin x2, other arithmetic, rotation(): return (jnp.cos(theta), jnp.sin(theta))  18.1 us
    unnamed x9, other arithmetic  9.09 us
  transfers between devices with their start and end apart: 18, of which 6 were waited for; matrix products, arithmetic and copies ran while one was open for 14% of the time, Pallas kernels for 12%

profile of v1, /device:TPU:10, one launch (start us, length us, event | category | flops | bytes accessed | tf_op | source)
XLA Modules:
  0.0 415.0 jit_solution(9248073857227126806)
XLA Ops:
  2.3 5.5 %fusion.56 = (f32[128,1024]{1,0:T(8,128)}, f32[128,1024]{1,0:T(8,128)}, bf16[128,1024]{1,0:T(8,128)(2,1)}, bf16[128,1024]{1,0:T(8,128)(2,1)}) fusion(s32[1024]{0:T(1024)S(1)} %copy-done.28, s32[128]{0:T(128)S(1)} %iota_multiply_fusion), kind=kLoop, calls=%fused_computation.226 | loop fusion | flops 3932160 | bytes 1577472 | tf_op jit(solution)/shard_map/sin | solution.py:81
  7.8 5.5 %spectrum.1 = bf16[2,16,1024]{2,1,0:T(8,128)(2,1)} custom-call(bf16[16,128,128]{2,1,0:T(8,128)(2,1)} %bitcast.394, bf16[128,1024]{1,0:T(8,128)(2,1)} %get-tuple-element.172.lc_ref, bf16[128,1024]{1,0:T(8,128)(2,1)} %get-tuple-element.171.ls_ref, f32[128,1024]{1,0:T(8,128)} %get-tuple-element.166.hc_ref, f32[128,1024]{1,0:T(8,128)} %get-tuple-element.165.hs_ref), custom_call_target="tpu_custom_call" | custom-call | flops 1073741824 | bytes 4194304 | tf_op jit(solution)/shard_map/spectrum/pallas_call | solution.py:71
  15.1 5.3 %all-to-all-start = ((bf16[4,2,16,1024]{3,1,2,0:T(2,128)(2,1)}), bf16[4,2,16,1024]{3,1,2,0:T(2,128)(2,1)}, u32[]{:S(2)}, u32[]{:S(2)}) async-start(bf16[4,2,16,1024]{3,1,2,0:T(2,128)(2,1)} %broadcast_in_dim.38), calls=%async_computation | async-start | bytes 524288 | tf_op jit(solution)/shard_map/all_to_all | solution.py:272
  20.5 5.3 %multiply_sine_fusion.1 = (f32[768,256]{1,0:T(8,128)}, f32[768,256]{1,0:T(8,128)}, f32[768,256]{1,0:T(8,128)}, f32[768,256]{1,0:T(8,128)}, f32[768,256]{1,0:T(8,...) fusion(f32[256]{0:T(256)S(1)} %convert_multiply_fusion.1, ...), kind=kLoop, calls=%fused_computation.48 | loop fusion | flops 6488064 | bytes 7868416 | tf_op jit(solution)/shard_map/sin | solution.py:240
  31.8 3.1 broadcast_select_fusion.mg_ref
  36.4 26.9 %block_ends.1 = (f32[4,2,768,256]{3,2,1,0:T(8,128)}, f32[4,2,768,256]{3,2,1,0:T(8,128)}) custom-call(bf16[32,768,64]{2,1,0:T(8,128)(2,1)} %broadcast_select_fusion.mg_ref, bf16[64,512]{1,0:T(8,128)(2,1)} %bitcast.400, f32[768,256]{1,0:T(8,128)} %get-tuple-element.162.c_ref, f32[768,256]{1,0:T(8,128)} %get-tuple-element.153.s_ref, f32[768,32]{1,0:T(8,128)} %bitcast.393, ...), custom_call_target="tpu_custom_call" | custom-call | flops 12884901888 | bytes 8388608 | tf_op jit(solution)/shard_map/block_ends/pallas_call | solution.py:128
  63.3 2.2 fusion
  68.0 3.9 collective-permute-start.7
  71.9 7.0 %collective-permute-done = bf16[2,768,256]{2,1,0:T(8,128)(2,1)S(1)} collective-permute-done((bf16[2,768,256]{2,1,0:T(8,128)(2,1)S(1)}, bf16[2,768,256]{2,1,0:T(8,128)(2,1)S(1)}, u32[]{:S(2)}, u32[]{:S(2)}) %collective-permute-start) | collective-permute-done | bytes 786464 | tf_op jit(solution)/shard_map/ppermute | solution.py:24
  79.6 6.0 %collective-permute-start.1 = (bf16[2,768,256]{2,1,0:T(8,128)(2,1)S(1)}, bf16[2,768,256]{2,1,0:T(8,128)(2,1)S(1)}, u32[]{:S(2)}, u32[]{:S(2)}) collective-permute-start(bf16[2,768,256]{2,1,0:T(8,128)(2,1)S(1)} %fusion.1), channel_id=1, source_target_pairs={{0,4},{4,8},{8,12},{12,16},{16,20},{20,24},{24,28},{1,5},{5,9},{9,... | collective-permute-start | bytes 2359304 | tf_op jit(solution)/shard_map/ppermute | solution.py:24
  87.0 3.8 collective-permute-start.8
  90.9 2.1 collective-permute-done.1
  93.6 12.8 %collective-permute-start.2 = (bf16[2,768,256]{2,1,0:T(8,128)(2,1)S(1)}, bf16[2,768,256]{2,1,0:T(8,128)(2,1)S(1)}, u32[]{:S(2)}, u32[]{:S(2)}) collective-permute-start(bf16[2,768,256]{2,1,0:T(8,128)(2,1)S(1)} %fusion.2), channel_id=1, source_target_pairs={{0,4},{4,8},{8,12},{12,16},{16,20},{20,24},{24,28},{1,5},{5,9},{9,... | collective-permute-start | bytes 2359304 | tf_op jit(solution)/shard_map/ppermute | solution.py:24
  107.0 3.7 collective-permute-start.9
  111.4 16.7 %collective-permute-start.3 = (bf16[2,768,256]{2,1,0:T(8,128)(2,1)S(1)}, bf16[2,768,256]{2,1,0:T(8,128)(2,1)S(1)}, u32[]{:S(2)}, u32[]{:S(2)}) collective-permute-start(bf16[2,768,256]{2,1,0:T(8,128)(2,1)S(1)} %fusion.3), channel_id=1, source_target_pairs={{0,4},{4,8},{8,12},{12,16},{16,20},{20,24},{24,28},{1,5},{5,9},{9,... | collective-permute-start | bytes 2359304 | tf_op jit(solution)/shard_map/ppermute | solution.py:24
  128.7 2.8 collective-permute-start.10
  132.1 18.7 %collective-permute-start.4 = (bf16[2,768,256]{2,1,0:T(8,128)(2,1)S(1)}, bf16[2,768,256]{2,1,0:T(8,128)(2,1)S(1)}, u32[]{:S(2)}, u32[]{:S(2)}) collective-permute-start(bf16[2,768,256]{2,1,0:T(8,128)(2,1)S(1)} %fusion.4), channel_id=1, source_target_pairs={{0,4},{4,8},{8,12},{12,16},{16,20},{20,24},{24,28},{1,5},{5,9},{9,... | collective-permute-start | bytes 2359304 | tf_op jit(solution)/shard_map/ppermute | solution.py:24
  154.0 19.8 %collective-permute-start.5 = (bf16[2,768,256]{2,1,0:T(8,128)(2,1)S(1)}, bf16[2,768,256]{2,1,0:T(8,128)(2,1)S(1)}, u32[]{:S(2)}, u32[]{:S(2)}) collective-permute-start(bf16[2,768,256]{2,1,0:T(8,128)(2,1)S(1)} %fusion.5), channel_id=1, source_target_pairs={{0,4},{4,8},{8,12},{12,16},{16,20},{20,24},{24,28},{1,5},{5,9},{9,... | collective-permute-start | bytes 2359304 | tf_op jit(solution)/shard_map/ppermute | solution.py:24
  177.0 20.0 %collective-permute-start.6 = (bf16[2,768,256]{2,1,0:T(8,128)(2,1)S(1)}, bf16[2,768,256]{2,1,0:T(8,128)(2,1)S(1)}, u32[]{:S(2)}, u32[]{:S(2)}) collective-permute-start(bf16[2,768,256]{2,1,0:T(8,128)(2,1)S(1)} %fusion.6), channel_id=1, source_target_pairs={{0,4},{4,8},{8,12},{12,16},{16,20},{20,24},{24,28},{1,5},{5,9},{9,... | collective-permute-start | bytes 2359304 | tf_op jit(solution)/shard_map/ppermute | solution.py:24
  197.7 2.1 collective-permute-start.13
  200.6 16.9 %collective-permute-done.13 = bf16[2,768,256]{2,1,0:T(8,128)(2,1)S(1)} collective-permute-done((bf16[2,768,256]{2,1,0:T(8,128)(2,1)S(1)}, bf16[2,768,256]{2,1,0:T(8,128)(2,1)S(1)}, u32[]{:S(2)}, u32[]{:S(2)}) %collective-permute-start.13) | collective-permute-done | bytes 786464 | tf_op jit(solution)/shard_map/ppermute | solution.py:24
  228.8 4.9 %all-to-all-start.2 = ((bf16[4,4,256,256]{3,2,1,0:T(8,128)(2,1)}), bf16[4,4,256,256]{3,2,1,0:T(8,128)(2,1)}, u32[]{:S(2)}, u32[]{:S(2)}) async-start(bf16[4,4,256,256]{3,2,1,0:T(8,128)(2,1)} %maximum_maximum_fusion.1), calls=%async_computation.2 | async-start | bytes 4194304 | tf_op jit(solution)/shard_map/all_to_all | solution.py:327
  234.0 2.1 fusion.54
  241.1 38.0 %all-to-all-done.2.in_ref = bf16[4,4,256,256]{3,2,1,0:T(8,128)(2,1)} async-done(((bf16[4,4,256,256]{3,2,1,0:T(8,128)(2,1)}), bf16[4,4,256,256]{3,2,1,0:T(8,128)(2,1)}, u32[]{:S(2)}, u32[]{:S(2)}) %all-to-all-start.2) | async-done | bytes 2097184 | tf_op jit(solution)/shard_map/all_to_all | solution.py:327
  279.2 7.8 %all-to-all-start.3 = ((bf16[4,4,256,256]{3,2,1,0:T(8,128)(2,1)}), bf16[4,4,256,256]{3,2,1,0:T(8,128)(2,1)}, u32[]{:S(2)}, u32[]{:S(2)}) async-start(bf16[4,4,256,256]{3,2,1,0:T(8,128)(2,1)} %maximum_maximum_fusion.2), calls=%async_computation.3 | async-start | bytes 4194304 | tf_op jit(solution)/shard_map/all_to_all | solution.py:327
  295.2 4.0 pad_maximum_fusion.inv_ref
  299.3 12.8 %multiply_sine_fusion = (f32[768,1024]{1,0:T(8,128)}, f32[768,1024]{1,0:T(8,128)}) fusion(f32[1024]{0:T(1024)S(1)} %convert_multiply_fusion, f32[768]{0:T(1024)S(1)} %copy-done.29), kind=kLoop, calls=%fused_computation.1 | loop fusion | flops 786432 | bytes 6298624 | tf_op jit(solution)/shard_map/sin | solution.py:240
  315.3 17.8 %all-to-all-done.3.in_ref = bf16[4,4,256,256]{3,2,1,0:T(8,128)(2,1)} async-done(((bf16[4,4,256,256]{3,2,1,0:T(8,128)(2,1)}), bf16[4,4,256,256]{3,2,1,0:T(8,128)(2,1)}, u32[]{:S(2)}, u32[]{:S(2)}) %all-to-all-start.3) | async-done | bytes 2097184 | tf_op jit(solution)/shard_map/all_to_all | solution.py:327
  333.1 7.0 %all-to-all-start.1 = ((bf16[4,4,256,256]{3,2,1,0:T(8,128)(2,1)}), bf16[4,4,256,256]{3,2,1,0:T(8,128)(2,1)S(1)}, u32[]{:S(2)}, u32[]{:S(2)}) async-start(bf16[4,4,256,256]{3,2,1,0:T(8,128)(2,1)} %maximum_maximum_fusion), calls=%async_computation.1 | async-start | bytes 4194304 | tf_op jit(solution)/shard_map/all_to_all | solution.py:327
  340.1 24.5 %march.3.rest_0_ = bf16[8,768,1024]{2,1,0:T(8,128)(2,1)} custom-call(bf16[8,768,64]{2,1,0:T(8,128)(2,1)} %broadcast_select_fusion.1.mg_ref, bf16[64,2048]{1,0:T(8,128)(2,1)} %bitcast.395, f32[768,1024]{1,0:T(8,128)} %get-tuple-element.152.c_ref, f32[768,1024]{1,0:T(8,128)} %get-tuple-element.151.s_ref, f32[768,8]{1,0:T(8,128)} %get-tuple-element.174.dd_ref, ...), custom_call_target="tpu_custom_call" | custom-call | flops 25769803776 | bytes 16777216 | tf_op jit(solution)/shard_map/march/pallas_call | solution.py:212
  364.5 24.5 %march.4.rest_0_ = bf16[8,768,1024]{2,1,0:T(8,128)(2,1)} custom-call(bf16[8,768,64]{2,1,0:T(8,128)(2,1)} %broadcast_select_fusion.1.mg_ref, bf16[64,2048]{1,0:T(8,128)(2,1)} %bitcast.396, f32[768,1024]{1,0:T(8,128)} %get-tuple-element.152.c_ref, f32[768,1024]{1,0:T(8,128)} %get-tuple-element.151.s_ref, ...), custom_call_target="tpu_custom_call", output_to_operand_aliasing={{}: (8, {})} | custom-call | flops 25769803776 | bytes 16777216 | tf_op jit(solution)/shard_map/march/pallas_call | solution.py:212
  390.5 24.5 %march.5 = bf16[8,768,1024]{2,1,0:T(8,128)(2,1)} custom-call(bf16[8,768,64]{2,1,0:T(8,128)(2,1)} %broadcast_select_fusion.1.mg_ref, bf16[64,2048]{1,0:T(8,128)(2,1)} %bitcast.397, f32[768,1024]{1,0:T(8,128)} %get-tuple-element.152.c_ref, f32[768,1024]{1,0:T(8,128)} %get-tuple-element.151.s_ref, ...), custom_call_target="tpu_custom_call", output_to_operand_aliasing={{}: (8, {})} | custom-call | flops 25769803776 | bytes 16777216 | tf_op jit(solution)/shard_map/march/pallas_call | solution.py:212
  (186 shorter events, 56.2 us)
Async XLA Ops:
  7.8 12.6 %copy-start.29 = (f32[768]{0:T(1024)S(1)}, f32[768]{0:T(1024)}, u32[]{:S(2)}) copy-start(f32[768]{0:T(1024)} %param.13) | copy-start | bytes 9220
  15.1 19.9 %all-to-all-start = ((bf16[4,2,16,1024]{3,1,2,0:T(2,128)(2,1)}), bf16[4,2,16,1024]{3,1,2,0:T(2,128)(2,1)}, u32[]{:S(2)}, u32[]{:S(2)}) async-start(bf16[4,2,16,1024]{3,1,2,0:T(2,128)(2,1)} %broadcast_in_dim.38), calls=%async_computation | async-start | bytes 524288 | tf_op jit(solution)/shard_map/all_to_all | solution.py:272
  65.5 13.4 %collective-permute-start = (bf16[2,768,256]{2,1,0:T(8,128)(2,1)S(1)}, bf16[2,768,256]{2,1,0:T(8,128)(2,1)S(1)}, u32[]{:S(2)}, u32[]{:S(2)}) collective-permute-start(bf16[2,768,256]{2,1,0:T(8,128)(2,1)S(1)} %fusion), channel_id=1, source_target_pairs={{0,4},{4,8},{8,12},{12,16},{16,20},{20,24},{24,28},{1,5},{5,9},{9,... | collective-permute-start | bytes 2359304 | tf_op jit(solution)/shard_map/ppermute | solution.py:24
  67.6 11.7 %slice-start = ((s8[6291456]{0:T(1024)(128)(4,1)}), s8[4194304]{0:T(1024)(128)(4,1)S(1)}, s32[]{:S(2)}) async-start(s8[6291456]{0:T(1024)(128)(4,1)} %bitcast.390), calls=%async_computation.4 | async-start | bytes 8388608
  67.7 11.6 %slice-start.1 = ((s8[6291456]{0:T(1024)(128)(4,1)}), s8[2097152]{0:T(1024)(128)(4,1)S(1)}, s32[]{:S(2)}) async-start(s8[6291456]{0:T(1024)(128)(4,1)} %bitcast.390), calls=%async_computation.5 | async-start | bytes 4194304
  68.0 18.4 %collective-permute-start.7 = (bf16[2,768,256]{2,1,0:T(8,128)(2,1)S(1)}, bf16[2,768,256]{2,1,0:T(8,128)(2,1)S(1)}, u32[]{:S(2)}, u32[]{:S(2)}) collective-permute-start(bf16[2,768,256]{2,1,0:T(8,128)(2,1)S(1)} %fusion.7), channel_id=1, source_target_pairs={{4,0},{8,4},{12,8},{16,12},{20,16},{24,20},{28,24},{5,1},{9,5},{13... | collective-permute-start | bytes 2359304 | tf_op jit(solution)/shard_map/ppermute | solution.py:24
  79.6 13.3 %collective-permute-start.1 = (bf16[2,768,256]{2,1,0:T(8,128)(2,1)S(1)}, bf16[2,768,256]{2,1,0:T(8,128)(2,1)S(1)}, u32[]{:S(2)}, u32[]{:S(2)}) collective-permute-start(bf16[2,768,256]{2,1,0:T(8,128)(2,1)S(1)} %fusion.1), channel_id=1, source_target_pairs={{0,4},{4,8},{8,12},{12,16},{16,20},{20,24},{24,28},{1,5},{5,9},{9,... | collective-permute-start | bytes 2359304 | tf_op jit(solution)/shard_map/ppermute | solution.py:24
  87.0 19.4 %collective-permute-start.8 = (bf16[2,768,256]{2,1,0:T(8,128)(2,1)S(1)}, bf16[2,768,256]{2,1,0:T(8,128)(2,1)S(1)}, u32[]{:S(2)}, u32[]{:S(2)}) collective-permute-start(bf16[2,768,256]{2,1,0:T(8,128)(2,1)S(1)} %fusion.8), channel_id=1, source_target_pairs={{4,0},{8,4},{12,8},{16,12},{20,16},{24,20},{28,24},{5,1},{9,5},{13... | collective-permute-start | bytes 2359304 | tf_op jit(solution)/shard_map/ppermute | solution.py:24
  93.6 17.1 %collective-permute-start.2 = (bf16[2,768,256]{2,1,0:T(8,128)(2,1)S(1)}, bf16[2,768,256]{2,1,0:T(8,128)(2,1)S(1)}, u32[]{:S(2)}, u32[]{:S(2)}) collective-permute-start(bf16[2,768,256]{2,1,0:T(8,128)(2,1)S(1)} %fusion.2), channel_id=1, source_target_pairs={{0,4},{4,8},{8,12},{12,16},{16,20},{20,24},{24,28},{1,5},{5,9},{9,... | collective-permute-start | bytes 2359304 | tf_op jit(solution)/shard_map/ppermute | solution.py:24
  107.0 21.0 %collective-permute-start.9 = (bf16[2,768,256]{2,1,0:T(8,128)(2,1)S(1)}, bf16[2,768,256]{2,1,0:T(8,128)(2,1)S(1)}, u32[]{:S(2)}, u32[]{:S(2)}) collective-permute-start(bf16[2,768,256]{2,1,0:T(8,128)(2,1)S(1)} %fusion.9), channel_id=1, source_target_pairs={{4,0},{8,4},{12,8},{16,12},{20,16},{24,20},{28,24},{5,1},{9,5},{13... | collective-permute-start | bytes 2359304 | tf_op jit(solution)/shard_map/ppermute | solution.py:24
  111.4 20.1 %collective-permute-start.3 = (bf16[2,768,256]{2,1,0:T(8,128)(2,1)S(1)}, bf16[2,768,256]{2,1,0:T(8,128)(2,1)S(1)}, u32[]{:S(2)}, u32[]{:S(2)}) collective-permute-start(bf16[2,768,256]{2,1,0:T(8,128)(2,1)S(1)} %fusion.3), channel_id=1, source_target_pairs={{0,4},{4,8},{8,12},{12,16},{16,20},{20,24},{24,28},{1,5},{5,9},{9,... | collective-permute-start | bytes 2359304 | tf_op jit(solution)/shard_map/ppermute | solution.py:24
  128.7 22.1 %collective-permute-start.10 = (bf16[2,768,256]{2,1,0:T(8,128)(2,1)S(1)}, bf16[2,768,256]{2,1,0:T(8,128)(2,1)S(1)}, u32[]{:S(2)}, u32[]{:S(2)}) collective-permute-start(bf16[2,768,256]{2,1,0:T(8,128)(2,1)S(1)} %fusion.10), channel_id=1, source_target_pairs={{4,0},{8,4},{12,8},{16,12},{20,16},{24,20},{28,24},{5,1},{9,5},{13... | collective-permute-start | bytes 2359304 | tf_op jit(solution)/shard_map/ppermute | solution.py:24
  132.1 21.2 %collective-permute-start.4 = (bf16[2,768,256]{2,1,0:T(8,128)(2,1)S(1)}, bf16[2,768,256]{2,1,0:T(8,128)(2,1)S(1)}, u32[]{:S(2)}, u32[]{:S(2)}) collective-permute-start(bf16[2,768,256]{2,1,0:T(8,128)(2,1)S(1)} %fusion.4), channel_id=1, source_target_pairs={{0,4},{4,8},{8,12},{12,16},{16,20},{20,24},{24,28},{1,5},{5,9},{9,... | collective-permute-start | bytes 2359304 | tf_op jit(solution)/shard_map/ppermute | solution.py:24
  151.4 22.4 %collective-permute-start.11 = (bf16[2,768,256]{2,1,0:T(8,128)(2,1)S(1)}, bf16[2,768,256]{2,1,0:T(8,128)(2,1)S(1)}, u32[]{:S(2)}, u32[]{:S(2)}) collective-permute-start(bf16[2,768,256]{2,1,0:T(8,128)(2,1)S(1)} %fusion.11), channel_id=1, source_target_pairs={{4,0},{8,4},{12,8},{16,12},{20,16},{24,20},{28,24},{5,1},{9,5},{13... | collective-permute-start | bytes 2359304 | tf_op jit(solution)/shard_map/ppermute | solution.py:24
  154.0 22.4 %collective-permute-start.5 = (bf16[2,768,256]{2,1,0:T(8,128)(2,1)S(1)}, bf16[2,768,256]{2,1,0:T(8,128)(2,1)S(1)}, u32[]{:S(2)}, u32[]{:S(2)}) collective-permute-start(bf16[2,768,256]{2,1,0:T(8,128)(2,1)S(1)} %fusion.5), channel_id=1, source_target_pairs={{0,4},{4,8},{8,12},{12,16},{16,20},{20,24},{24,28},{1,5},{5,9},{9,... | collective-permute-start | bytes 2359304 | tf_op jit(solution)/shard_map/ppermute | solution.py:24
  174.4 22.6 %collective-permute-start.12 = (bf16[2,768,256]{2,1,0:T(8,128)(2,1)S(1)}, bf16[2,768,256]{2,1,0:T(8,128)(2,1)S(1)}, u32[]{:S(2)}, u32[]{:S(2)}) collective-permute-start(bf16[2,768,256]{2,1,0:T(8,128)(2,1)S(1)} %fusion.12), channel_id=1, source_target_pairs={{4,0},{8,4},{12,8},{16,12},{20,16},{24,20},{28,24},{5,1},{9,5},{13... | collective-permute-start | bytes 2359304 | tf_op jit(solution)/shard_map/ppermute | solution.py:24
  177.0 22.9 %collective-permute-start.6 = (bf16[2,768,256]{2,1,0:T(8,128)(2,1)S(1)}, bf16[2,768,256]{2,1,0:T(8,128)(2,1)S(1)}, u32[]{:S(2)}, u32[]{:S(2)}) collective-permute-start(bf16[2,768,256]{2,1,0:T(8,128)(2,1)S(1)} %fusion.6), channel_id=1, source_target_pairs={{0,4},{4,8},{8,12},{12,16},{16,20},{20,24},{24,28},{1,5},{5,9},{9,... | collective-permute-start | bytes 2359304 | tf_op jit(solution)/shard_map/ppermute | solution.py:24
  197.7 19.8 %collective-permute-start.13 = (bf16[2,768,256]{2,1,0:T(8,128)(2,1)S(1)}, bf16[2,768,256]{2,1,0:T(8,128)(2,1)S(1)}, u32[]{:S(2)}, u32[]{:S(2)}) collective-permute-start(bf16[2,768,256]{2,1,0:T(8,128)(2,1)S(1)} %fusion.13), channel_id=1, source_target_pairs={{4,0},{8,4},{12,8},{16,12},{20,16},{24,20},{28,24},{5,1},{9,5},{13... | collective-permute-start | bytes 2359304 | tf_op jit(solution)/shard_map/ppermute | solution.py:24
  200.6 17.0 %copy-start.1 = (f32[768,256]{1,0:T(8,128)S(1)}, f32[768,256]{1,0:T(8,128)}, u32[]{:S(2)}) copy-start(f32[768,256]{1,0:T(8,128)} %get-tuple-element.28) | copy-start | bytes 2359300
  200.6 17.0 %copy-start.2 = (f32[768,256]{1,0:T(8,128)S(1)}, f32[768,256]{1,0:T(8,128)}, u32[]{:S(2)}) copy-start(f32[768,256]{1,0:T(8,128)} %get-tuple-element.32) | copy-start | bytes 2359300
  228.8 7.3 %copy-start.9 = (f32[32,768]{0,1:T(8,128)S(1)}, f32[32,768]{0,1:T(8,128)}, u32[]{:S(2)}) copy-start(f32[32,768]{0,1:T(8,128)} %copy.19) | copy-start | bytes 294916
  228.8 50.3 %all-to-all-start.2 = ((bf16[4,4,256,256]{3,2,1,0:T(8,128)(2,1)}), bf16[4,4,256,256]{3,2,1,0:T(8,128)(2,1)}, u32[]{:S(2)}, u32[]{:S(2)}) async-start(bf16[4,4,256,256]{3,2,1,0:T(8,128)(2,1)} %maximum_maximum_fusion.1), calls=%async_computation.2 | async-start | bytes 4194304 | tf_op jit(solution)/shard_map/all_to_all | solution.py:327
  279.2 53.9 %all-to-all-start.3 = ((bf16[4,4,256,256]{3,2,1,0:T(8,128)(2,1)}), bf16[4,4,256,256]{3,2,1,0:T(8,128)(2,1)}, u32[]{:S(2)}, u32[]{:S(2)}) async-start(bf16[4,4,256,256]{3,2,1,0:T(8,128)(2,1)} %maximum_maximum_fusion.2), calls=%async_computation.3 | async-start | bytes 4194304 | tf_op jit(solution)/shard_map/all_to_all | solution.py:327
  299.2 14.5 %copy-start.12 = (bf16[1,2,256,256]{3,2,1,0:T(8,128)(2,1)S(1)}, bf16[1,2,256,256]{3,2,1,0:T(8,128)(2,1)}, u32[]{:S(2)}) copy-start(bf16[1,2,256,256]{3,2,1,0:T(8,128)(2,1)} %get-tuple-element.127) | copy-start | bytes 786436
  299.2 14.6 %copy-start.13 = (bf16[1,2,256,256]{3,2,1,0:T(8,128)(2,1)S(1)}, bf16[1,2,256,256]{3,2,1,0:T(8,128)(2,1)}, u32[]{:S(2)}) copy-start(bf16[1,2,256,256]{3,2,1,0:T(8,128)(2,1)} %get-tuple-element.124) | copy-start | bytes 786436
  299.2 14.6 %copy-start.14 = (bf16[1,2,256,256]{3,2,1,0:T(8,128)(2,1)S(1)}, bf16[1,2,256,256]{3,2,1,0:T(8,128)(2,1)}, u32[]{:S(2)}) copy-start(bf16[1,2,256,256]{3,2,1,0:T(8,128)(2,1)} %get-tuple-element.121) | copy-start | bytes 786436
  299.2 14.6 %copy-start.15 = (bf16[1,2,256,256]{3,2,1,0:T(8,128)(2,1)S(1)}, bf16[1,2,256,256]{3,2,1,0:T(8,128)(2,1)}, u32[]{:S(2)}) copy-start(bf16[1,2,256,256]{3,2,1,0:T(8,128)(2,1)} %get-tuple-element.118) | copy-start | bytes 786436
  299.2 14.6 %copy-start.16 = (bf16[1,2,256,256]{3,2,1,0:T(8,128)(2,1)S(1)}, bf16[1,2,256,256]{3,2,1,0:T(8,128)(2,1)}, u32[]{:S(2)}) copy-start(bf16[1,2,256,256]{3,2,1,0:T(8,128)(2,1)} %get-tuple-element.115) | copy-start | bytes 786436
  299.3 14.6 %copy-start.17 = (bf16[1,2,256,256]{3,2,1,0:T(8,128)(2,1)S(1)}, bf16[1,2,256,256]{3,2,1,0:T(8,128)(2,1)}, u32[]{:S(2)}) copy-start(bf16[1,2,256,256]{3,2,1,0:T(8,128)(2,1)} %get-tuple-element.112) | copy-start | bytes 786436
  299.3 14.6 %copy-start.18 = (bf16[1,2,256,256]{3,2,1,0:T(8,128)(2,1)S(1)}, bf16[1,2,256,256]{3,2,1,0:T(8,128)(2,1)}, u32[]{:S(2)}) copy-start(bf16[1,2,256,256]{3,2,1,0:T(8,128)(2,1)} %get-tuple-element.130) | copy-start | bytes 786436
  299.3 14.6 %copy-start.19 = (bf16[1,2,256,256]{3,2,1,0:T(8,128)(2,1)S(1)}, bf16[1,2,256,256]{3,2,1,0:T(8,128)(2,1)}, u32[]{:S(2)}) copy-start(bf16[1,2,256,256]{3,2,1,0:T(8,128)(2,1)} %get-tuple-element.109) | copy-start | bytes 786436
  333.1 56.0 %all-to-all-start.1 = ((bf16[4,4,256,256]{3,2,1,0:T(8,128)(2,1)}), bf16[4,4,256,256]{3,2,1,0:T(8,128)(2,1)S(1)}, u32[]{:S(2)}, u32[]{:S(2)}) async-start(bf16[4,4,256,256]{3,2,1,0:T(8,128)(2,1)} %maximum_maximum_fusion), calls=%async_computation.1 | async-start | bytes 4194304 | tf_op jit(solution)/shard_map/all_to_all | solution.py:327
  (19 other events, 56.3 us)

commit v2 on v1

--- a/solution.py
+++ b/solution.py
@@ -16,12 +16,6 @@
 SUB = 16
 F32 = jnp.float32
 BF16 = jnp.bfloat16
-
-
-def shifted(block, axis, distance):
-    devices = range(lax.axis_size(axis))
-    route = [(i - distance, i) for i in devices if i - distance in devices]
-    return lax.ppermute(block, axis, route)
 
 
 def cmul(left, right):
@@ -144,6 +138,97 @@
         ),
         name="block_ends",
     )(mg, spec, c, s, dd, du)
+
+
+def relay_kernel(
+    fac_down, last_down, fac_up, last_up, below, above, out_down, out_up, sd, rd, su, ru
+):
+    n, me = lax.axis_size("st"), lax.axis_index("st")
+    right, left = lax.rem(me + 1, n), lax.rem(me + n - 1, n)
+    count = below.shape[1] // TILE
+    barrier = pltpu.get_barrier_semaphore()
+    for neighbour in (left, right):
+        pl.semaphore_signal(
+            barrier, inc=1, device_id={"st": neighbour}, device_id_type=pl.DeviceIdType.MESH
+        )
+    pl.semaphore_wait(barrier, 2)
+
+    def rows_of(p):
+        return pl.ds(pl.multiple_of(p * TILE, TILE), TILE)
+
+    def copy(p, source, target, send, recv, device):
+        return pltpu.make_async_remote_copy(
+            src_ref=source.at[:, rows_of(p), :],
+            dst_ref=target.at[:, rows_of(p), :],
+            send_sem=send.at[p],
+            recv_sem=recv.at[p],
+            device_id={"st": device},
+            device_id_type=pl.DeviceIdType.MESH,
+        )
+
+    def down_copy(p):
+        return copy(p, out_down, below, sd, rd, right)
+
+    def up_copy(p):
+        return copy(p, out_up, above, su, ru, left)
+
+    def visit(p, first, final, moved, entering, factor, last, leaving):
+        @pl.when((p >= 0) & (p < count))
+        def _():
+            rows = rows_of(p)
+
+            @pl.when(first)
+            def _():
+                entering[:, rows, :] = jnp.zeros((2, TILE, entering.shape[2]), BF16)
+
+            @pl.when(jnp.logical_not(first))
+            def _():
+                moved(p).wait_recv()
+
+            @pl.when(jnp.logical_not(final))
+            def _():
+                state = (entering[0, rows, :].astype(F32), entering[1, rows, :].astype(F32))
+                re, im = cmul((factor[0, rows, :], factor[1, rows, :]), state)
+                leaving[0, rows, :] = (re + last[0, rows, :]).astype(BF16)
+                leaving[1, rows, :] = (im + last[1, rows, :]).astype(BF16)
+                moved(p).start()
+
+    def turn(t, unused):
+        bottom, top = me == 0, me == n - 1
+        visit(t - me, bottom, top, down_copy, below, fac_down, last_down, out_down)
+        visit(t - (n - 1 - me), top, bottom, up_copy, above, fac_up, last_up, out_up)
+        return unused
+
+    lax.fori_loop(0, n - 1 + count, turn, 0)
+
+    def finish(p, unused):
+        @pl.when(me < n - 1)
+        def _():
+            down_copy(p).wait_send()
+
+        @pl.when(me > 0)
+        def _():
+            up_copy(p).wait_send()
+
+        return unused
+
+    lax.fori_loop(0, count, finish, 0)
+
+
+def relay(fac_down, last_down, fac_up, last_up):
+    _, width, fd = last_down.shape
+    vmem = pl.BlockSpec(memory_space=pltpu.VMEM)
+    out = jax.ShapeDtypeStruct((2, width, fd), BF16)
+    sems = pltpu.SemaphoreType.DMA((width // TILE,))
+    return pl.pallas_call(
+        relay_kernel,
+        in_specs=[vmem] * 4,
+        out_specs=[vmem] * 2,
+        out_shape=[out, out],
+        scratch_shapes=[pltpu.VMEM((2, width, fd), BF16)] * 2 + [sems] * 4,
+        compiler_params=pltpu.CompilerParams(collective_id=0, has_side_effects=True),
+        name="relay",
+    )(fac_down, last_down, fac_up, last_up)
 
 
 def march_kernel(mg_ref, spec_ref, c_ref, s_ref, dd_ref, du_ref, in_ref, inv_ref, *rest):
@@ -305,14 +390,16 @@
         rate = jnp.prod(damping_up[st_dev - j * own :], axis=0)[:, None]
         return (rate * turns[j - 1][0], rate * turns[j - 1][1])
 
-    full_down, full_up = lax.optimization_barrier((down_factor(parts), up_factor(parts)))
-    below = above = jnp.zeros((2, width, fd), F32)
-    for hop in range(lax.axis_size("st") - 1):
-        out_down = jnp.stack(cmul(full_down, below)) + down_loc[parts - 1]
-        out_up = jnp.stack(cmul(full_up, above)) + up_loc[parts - 1]
-        below = shifted(out_down.astype(BF16), "st", 1).astype(F32)
-        above = shifted(out_up.astype(BF16), "st", -1).astype(F32)
+    full_down, full_up = jnp.stack(down_factor(parts)), jnp.stack(up_factor(parts))
+    below, above = relay(full_down, down_loc[parts - 1], full_up, up_loc[parts - 1])
+    below, above = below.astype(F32), above.astype(F32)
+    def march(i, filled):
+        return estimate_chunk(
+            i, mg_own, spec, c_all, s_all, dd_own, du_own, entering[i], inverse, filled
+        )
+
     entering = []
+    result = None
     for i in range(CHUNKS):
         rows = slice(i * chunk_width, (i + 1) * chunk_width)
         pieces = []
@@ -324,13 +411,18 @@
                 lifted = jnp.stack(cmul(up_factor(parts - 1 - q), above))
                 up_in = (lifted + up_loc[parts - 2 - q])[:, rows]
             pieces.append(jnp.concatenate([down_in, up_in], axis=0).astype(BF16))
-        entering.append(lax.all_to_all(jnp.stack(pieces), "fq", 0, 0, tiled=True))
-
-    result = None
-    for i in range(CHUNKS):
-        result = estimate_chunk(
-            i, mg_own, spec, c_all, s_all, dd_own, du_own, entering[i], inverse, result
-        )
+        leaving = jnp.stack(pieces)
+        if i == 1:
+            leaving, c_all, s_all, inverse = lax.optimization_barrier(
+                (leaving, c_all, s_all, inverse)
+            )
+        if i >= 2:
+            result = march(i - 2, result)
+            leaving, result = lax.optimization_barrier((leaving, result))
+        entering.append(lax.all_to_all(leaving, "fq", 0, 0, tiled=True))
+
+    for i in range(max(CHUNKS - 2, 0), CHUNKS):
+        result = march(i, result)
     return result
 
 

time: 416 us -> 320 us (0.77)
  the two profiles are of different devices: /device:TPU:10 before, /device:TPU:0 now
where the time goes in v2:
time: 320 us; the launch traced here: 319 us
  Pallas kernels  144 us (45%)
  other arithmetic  63 us (20%)
  waiting for transfers between devices  62.9 us (20%)
  local copies, waits for them, and re-layouts  28.5 us (9%)
  starting transfers between devices  19.2 us (6%)
    pallas_call x3, Pallas kernels, estimate_chunk(): pl.pallas_call(march_kernel, grid=(tiles,), in_specs=specs, out_specs=pl....  73.5 us
    all_to_all x3, waiting for transfers between devices, on_device(): entering.append(lax.all_to_all(leaving, 'fq', 0, 0, tiled=True))  62.9 us
    pallas_call x1, Pallas kernels, relay(): pl.pallas_call(relay_kernel, in_specs=[vmem] * 4, out_specs=[vmem] * 2, o...  38.5 us
    pallas_call x1, Pallas kernels, block_ends(): pl.pallas_call(functools.partial(ends_kernel, own), grid=(tiles,), in_spe...  26.8 us
    sin x2, other arithmetic, rotation(): return (jnp.cos(theta), jnp.sin(theta))  18.5 us
    all_to_all x3, starting transfers between devices, on_device(): entering.append(lax.all_to_all(leaving, 'fq', 0, 0, tiled=True))  12.9 us
    unnamed x103, local copies, waits for them, and re-layouts  10.3 us
    unnamed x10, other arithmetic  9.4 us
  transfers between devices with their start and end apart: 4, of which 3 were waited for; matrix products, arithmetic and copies ran while one was open for 18% of the time, Pallas kernels for 15%

profile of v2, /device:TPU:0, one launch (start us, length us, event | category | flops | bytes accessed | tf_op | source)
XLA Modules:
  0.0 318.7 jit_solution(5438949853303721252)
XLA Ops:
  2.3 5.5 %fusion.42 = (f32[128,1024]{1,0:T(8,128)}, f32[128,1024]{1,0:T(8,128)}, bf16[128,1024]{1,0:T(8,128)(2,1)}, bf16[128,1024]{1,0:T(8,128)(2,1)}) fusion(s32[1024]{0:T(1024)S(1)} %copy-done.27, s32[128]{0:T(128)S(1)} %iota_multiply_fusion), kind=kLoop, calls=%fused_computation.150 | loop fusion | flops 3932160 | bytes 1577472 | tf_op jit(solution)/shard_map/sin | solution.py:75
  7.8 5.5 %spectrum.1 = bf16[2,16,1024]{2,1,0:T(8,128)(2,1)} custom-call(bf16[16,128,128]{2,1,0:T(8,128)(2,1)} %bitcast.192, bf16[128,1024]{1,0:T(8,128)(2,1)} %get-tuple-element.152.lc_ref, bf16[128,1024]{1,0:T(8,128)(2,1)} %get-tuple-element.151.ls_ref, f32[128,1024]{1,0:T(8,128)} %get-tuple-element.146.hc_ref, f32[128,1024]{1,0:T(8,128)} %get-tuple-element.145.hs_ref), custom_call_target="tpu_custom_call" | custom-call | flops 1073741824 | bytes 4194304 | tf_op jit(solution)/shard_map/spectrum/pallas_call | solution.py:65
  15.2 6.3 %all-to-all-start = ((bf16[4,2,16,1024]{3,1,2,0:T(2,128)(2,1)}), bf16[4,2,16,1024]{3,1,2,0:T(2,128)(2,1)}, u32[]{:S(2)}, u32[]{:S(2)}) async-start(bf16[4,2,16,1024]{3,1,2,0:T(2,128)(2,1)} %broadcast_in_dim.38), calls=%async_computation | async-start | bytes 524288 | tf_op jit(solution)/shard_map/all_to_all | solution.py:357
  24.0 2.1 fusion.40
  28.9 5.7 %multiply_sine_fusion.1 = (f32[768,256]{1,0:T(8,128)}, f32[768,256]{1,0:T(8,128)S(1)}, f32[768,256]{1,0:T(8,128)}, f32[768,256]{1,0:T(8,128)S(1)}, f32[768,256]{...) fusion(f32[256]{0:T(256)} %convert_multiply_fusion.1, ...), kind=kLoop, calls=%fused_computation.24 | loop fusion | flops 6488064 | bytes 7868416 | tf_op jit(solution)/shard_map/sin | solution.py:325
  35.0 1.2 pad_maximum_fusion.2.fac_up
  36.3 1.3 pad_maximum_fusion.1.fac_down
  40.2 1.8 copy.21
  42.1 1.7 copy.17
  43.8 4.0 %broadcast_select_fusion.mg_ref = bf16[32,768,64]{2,1,0:T(8,128)(2,1)} fusion(pred[32,64]{1,0:T(8,128)(4,1)} %iota_compare_fusion, bf16[768,64]{1,0:T(8,128)(2,1)} %copy.17), kind=kLoop, calls=%fused_computation | loop fusion | flops 1572864 | bytes 3246080 | tf_op jit(solution)/shard_map/jit(_where)/select_n | solution.py:319
  49.3 26.8 %block_ends.1 = (f32[4,2,768,256]{3,2,1,0:T(8,128)}, f32[4,2,768,256]{3,2,1,0:T(8,128)}) custom-call(bf16[32,768,64]{2,1,0:T(8,128)(2,1)} %broadcast_select_fusion.mg_ref, bf16[64,512]{1,0:T(8,128)(2,1)} %bitcast.198, f32[768,256]{1,0:T(8,128)} %get-tuple-element.142.c_ref, f32[768,256]{1,0:T(8,128)} %get-tuple-element.133.s_ref, f32[768,32]{1,0:T(8,128)} %bitcast.190, ...), custom_call_target="tpu_custom_call" | custom-call | flops 12884901888 | bytes 8388608 | tf_op jit(solution)/shard_map/block_ends/pallas_call | solution.py:122
  76.2 2.7 slice_bitcast_fusion.1.last_down
  78.8 2.7 slice_bitcast_fusion.last_up
  81.5 38.5 %relay.1 = (bf16[2,768,256]{2,1,0:T(8,128)(2,1)}, bf16[2,768,256]{2,1,0:T(8,128)(2,1)}) custom-call(f32[2,768,256]{2,1,0:T(8,128)} %pad_maximum_fusion.1.fac_down, f32[2,768,256]{2,1,0:T(8,128)} %slice_bitcast_fusion.1.last_down, f32[2,768,256]{2,1,0:T(8,128)} %pad_maximum_fusion.2.fac_up, f32[2,768,256]{2,1,0:T(8,128)} %slice_bitcast_fusion.last_up), custom_call_target="tpu_custom_call" | custom-call | tf_op jit(solution)/shard_map/relay/pallas_call | solution.py:223
  120.1 1.4 convert_element_type.196
  134.0 1.4 maximum_maximum_fusion.2
  135.5 4.9 %all-to-all-start.1 = ((bf16[4,4,256,256]{3,2,1,0:T(8,128)(2,1)}), bf16[4,4,256,256]{3,2,1,0:T(8,128)(2,1)}, u32[]{:S(2)}, u32[]{:S(2)}) async-start(bf16[4,4,256,256]{3,2,1,0:T(8,128)(2,1)} %maximum_maximum_fusion.2), calls=%async_computation.1 | async-start | bytes 4194304 | tf_op jit(solution)/shard_map/all_to_all | solution.py:422
  148.8 4.0 %pad_maximum_fusion.inv_ref = bf16[2048,1024]{1,0:T(8,128)(2,1)} fusion(bf16[1024,1024]{1,0:T(8,128)(2,1)} %get-tuple-element.72, bf16[1024,1024]{1,0:T(8,128)(2,1)S(1)} %get-tuple-element.71), kind=kLoop, calls=%fused_computation.3 | loop fusion | flops 8388608 | bytes 8388608 | tf_op jit(solution)/shard_map/concatenate | solution.py:343
  152.8 12.8 %multiply_sine_fusion = (f32[768,1024]{1,0:T(8,128)}, f32[768,1024]{1,0:T(8,128)}) fusion(f32[1024]{0:T(1024)S(1)} %copy-done.38, f32[768]{0:T(1024)S(1)} %copy-done.28), kind=kLoop, calls=%fused_computation.1 | loop fusion | flops 786432 | bytes 6298624 | tf_op jit(solution)/shard_map/sin | solution.py:325
  165.7 1.4 maximum_maximum_fusion
  167.1 22.0 %all-to-all-done.1.in_ref = bf16[4,4,256,256]{3,2,1,0:T(8,128)(2,1)} async-done(((bf16[4,4,256,256]{3,2,1,0:T(8,128)(2,1)}), bf16[4,4,256,256]{3,2,1,0:T(8,128)(2,1)}, u32[]{:S(2)}, u32[]{:S(2)}) %all-to-all-start.1) | async-done | bytes 2097184 | tf_op jit(solution)/shard_map/all_to_all | solution.py:422
  189.2 3.6 %all-to-all-start.3 = ((bf16[4,4,256,256]{3,2,1,0:T(8,128)(2,1)}), bf16[4,4,256,256]{3,2,1,0:T(8,128)(2,1)S(1)}, u32[]{:S(2)}, u32[]{:S(2)}) async-start(bf16[4,4,256,256]{3,2,1,0:T(8,128)(2,1)} %maximum_maximum_fusion), calls=%async_computation.3 | async-start | bytes 4194304 | tf_op jit(solution)/shard_map/all_to_all | solution.py:422
  194.1 1.3 broadcast_select_fusion.1.mg_ref
  195.3 1.7 copy.25
  197.1 1.4 maximum_maximum_fusion.1
  198.5 24.5 %march.3.rest_0_ = bf16[8,768,1024]{2,1,0:T(8,128)(2,1)} custom-call(bf16[8,768,64]{2,1,0:T(8,128)(2,1)} %broadcast_select_fusion.1.mg_ref, bf16[64,2048]{1,0:T(8,128)(2,1)} %bitcast.193, f32[768,1024]{1,0:T(8,128)} %get-tuple-element.43.c_ref, f32[768,1024]{1,0:T(8,128)} %get-tuple-element.44.s_ref, f32[768,8]{1,0:T(8,128)} %get-tuple-element.161.dd_ref, ...), custom_call_target="tpu_custom_call" | custom-call | flops 25769803776 | bytes 16777216 | tf_op jit(solution)/shard_map/march/pallas_call | solution.py:297
  223.0 17.6 %all-to-all-done.3.in_ref = bf16[4,4,256,256]{3,2,1,0:T(8,128)(2,1)S(1)} async-done(((bf16[4,4,256,256]{3,2,1,0:T(8,128)(2,1)}), bf16[4,4,256,256]{3,2,1,0:T(8,128)(2,1)S(1)}, u32[]{:S(2)}, u32[]{:S(2)}) %all-to-all-start.3) | async-done | bytes 2097184 | tf_op jit(solution)/shard_map/all_to_all | solution.py:422
  240.6 1.3 copy-done.6
  241.9 4.4 %all-to-all-start.2 = ((bf16[4,4,256,256]{3,2,1,0:T(8,128)(2,1)}), bf16[4,4,256,256]{3,2,1,0:T(8,128)(2,1)}, u32[]{:S(2)}, u32[]{:S(2)}) async-start(bf16[4,4,256,256]{3,2,1,0:T(8,128)(2,1)} %maximum_maximum_fusion.1), calls=%async_computation.2 | async-start | bytes 4194304 | tf_op jit(solution)/shard_map/all_to_all | solution.py:422
  246.4 24.5 %march.4.rest_0_ = bf16[8,768,1024]{2,1,0:T(8,128)(2,1)} custom-call(bf16[8,768,64]{2,1,0:T(8,128)(2,1)} %broadcast_select_fusion.1.mg_ref, bf16[64,2048]{1,0:T(8,128)(2,1)} %bitcast.194, f32[768,1024]{1,0:T(8,128)} %get-tuple-element.43.c_ref, f32[768,1024]{1,0:T(8,128)} %get-tuple-element.44.s_ref, ...), custom_call_target="tpu_custom_call", output_to_operand_aliasing={{}: (8, {})} | custom-call | flops 25769803776 | bytes 16777216 | tf_op jit(solution)/shard_map/march/pallas_call | solution.py:297
  270.9 23.3 %all-to-all-done.2.in_ref = bf16[4,4,256,256]{3,2,1,0:T(8,128)(2,1)} async-done(((bf16[4,4,256,256]{3,2,1,0:T(8,128)(2,1)}), bf16[4,4,256,256]{3,2,1,0:T(8,128)(2,1)}, u32[]{:S(2)}, u32[]{:S(2)}) %all-to-all-start.2) | async-done | bytes 2097184 | tf_op jit(solution)/shard_map/all_to_all | solution.py:422
  294.2 24.5 %march.5 = bf16[8,768,1024]{2,1,0:T(8,128)(2,1)} custom-call(bf16[8,768,64]{2,1,0:T(8,128)(2,1)} %broadcast_select_fusion.1.mg_ref, bf16[64,2048]{1,0:T(8,128)(2,1)} %bitcast.195, f32[768,1024]{1,0:T(8,128)} %get-tuple-element.43.c_ref, f32[768,1024]{1,0:T(8,128)} %get-tuple-element.44.s_ref, ...), custom_call_target="tpu_custom_call", output_to_operand_aliasing={{}: (8, {})} | custom-call | flops 25769803776 | bytes 16777216 | tf_op jit(solution)/shard_map/march/pallas_call | solution.py:297
  (155 shorter events, 36.0 us)
Async XLA Ops:
  7.8 13.7 %copy-start.10 = (f32[32,768]{1,0:T(8,128)S(1)}, f32[32,768]{1,0:T(8,128)}, u32[]{:S(2)}) copy-start(f32[32,768]{1,0:T(8,128)} %param.11) | copy-start | bytes 294916
  7.8 14.4 %copy-start.11 = (f32[32,768]{1,0:T(8,128)S(1)}, f32[32,768]{1,0:T(8,128)}, u32[]{:S(2)}) copy-start(f32[32,768]{1,0:T(8,128)} %param.12) | copy-start | bytes 294916
  13.3 13.5 %copy-start.44 = (s32[64]{0:T(128)S(1)}, s32[64]{0:T(128)}, u32[]{:S(2)}) copy-start(s32[64]{0:T(128)} %param.9) | copy-start | bytes 772
  13.3 15.6 %copy-start.28 = (f32[768]{0:T(1024)S(1)}, f32[768]{0:T(1024)}, u32[]{:S(2)}) copy-start(f32[768]{0:T(1024)} %param.13) | copy-start | bytes 9220
  15.2 32.7 %all-to-all-start = ((bf16[4,2,16,1024]{3,1,2,0:T(2,128)(2,1)}), bf16[4,2,16,1024]{3,1,2,0:T(2,128)(2,1)}, u32[]{:S(2)}, u32[]{:S(2)}) async-start(bf16[4,2,16,1024]{3,1,2,0:T(2,128)(2,1)} %broadcast_in_dim.38), calls=%async_computation | async-start | bytes 524288 | tf_op jit(solution)/shard_map/all_to_all | solution.py:357
  28.9 5.7 %copy-start.40 = (f32[768]{0:T(1024)S(1)}, f32[768]{0:T(1024)}, u32[]{:S(2)}) copy-start(f32[768]{0:T(1024)} %reduce_prod.71) | copy-start | bytes 9220
  135.5 4.9 %copy-start.42 = (s32[64]{0:T(128)S(1)}, s32[64]{0:T(128)}, u32[]{:S(2)}) copy-start(s32[64]{0:T(128)} %copy-done.41) | copy-start | bytes 772
  135.5 4.9 %copy-start.43 = (s32[8]{0:T(128)S(1)}, s32[8]{0:T(128)}, u32[]{:S(2)}) copy-start(s32[8]{0:T(128)} %iota_add_fusion) | copy-start | bytes 100
  135.5 5.0 %copy-start.5 = (bf16[1024,1024]{1,0:T(8,128)(2,1)S(1)}, bf16[1024,1024]{1,0:T(8,128)(2,1)}, u32[]{:S(2)}) copy-start(bf16[1024,1024]{1,0:T(8,128)(2,1)} %get-tuple-element.85) | copy-start | bytes 6291460
  135.5 5.0 %copy-start.34 = (f32[1024,1]{0,1:T(1,128)S(1)}, f32[1024,1]{0,1:T(1,128)}, u32[]{:S(2)}) copy-start(f32[1024,1]{0,1:T(1,128)} %get-tuple-element.129) | copy-start | bytes 12292
  135.5 5.0 %copy-start.36 = (f32[1024,1]{0,1:T(1,128)S(1)}, f32[1024,1]{0,1:T(1,128)}, u32[]{:S(2)}) copy-start(f32[1024,1]{0,1:T(1,128)} %get-tuple-element.121) | copy-start | bytes 12292
  135.5 6.2 %copy-start.32 = (f32[1024,1]{0,1:T(1,128)S(1)}, f32[1024,1]{0,1:T(1,128)}, u32[]{:S(2)}) copy-start(f32[1024,1]{0,1:T(1,128)} %get-tuple-element.128) | copy-start | bytes 12292
  135.5 6.2 %copy-start.35 = (f32[1024,1]{0,1:T(1,128)S(1)}, f32[1024,1]{0,1:T(1,128)}, u32[]{:S(2)}) copy-start(f32[1024,1]{0,1:T(1,128)} %get-tuple-element.120) | copy-start | bytes 12292
  135.5 53.7 %all-to-all-start.1 = ((bf16[4,4,256,256]{3,2,1,0:T(8,128)(2,1)}), bf16[4,4,256,256]{3,2,1,0:T(8,128)(2,1)}, u32[]{:S(2)}, u32[]{:S(2)}) async-start(bf16[4,4,256,256]{3,2,1,0:T(8,128)(2,1)} %maximum_maximum_fusion.2), calls=%async_computation.1 | async-start | bytes 4194304 | tf_op jit(solution)/shard_map/all_to_all | solution.py:422
  152.8 12.9 %copy-start.14 = (bf16[1,2,256,256]{3,2,1,0:T(8,128)(2,1)S(1)}, bf16[1,2,256,256]{3,2,1,0:T(8,128)(2,1)}, u32[]{:S(2)}) copy-start(bf16[1,2,256,256]{3,2,1,0:T(8,128)(2,1)} %get-tuple-element.110) | copy-start | bytes 786436
  152.8 12.9 %copy-start.15 = (bf16[1,2,256,256]{3,2,1,0:T(8,128)(2,1)S(1)}, bf16[1,2,256,256]{3,2,1,0:T(8,128)(2,1)}, u32[]{:S(2)}) copy-start(bf16[1,2,256,256]{3,2,1,0:T(8,128)(2,1)} %get-tuple-element.155) | copy-start | bytes 786436
  152.8 12.9 %copy-start.18 = (bf16[1,2,256,256]{3,2,1,0:T(8,128)(2,1)S(1)}, bf16[1,2,256,256]{3,2,1,0:T(8,128)(2,1)}, u32[]{:S(2)}) copy-start(bf16[1,2,256,256]{3,2,1,0:T(8,128)(2,1)} %get-tuple-element.95) | copy-start | bytes 786436
  152.8 12.9 %copy-start.22 = (bf16[1,2,256,256]{3,2,1,0:T(8,128)(2,1)S(1)}, bf16[1,2,256,256]{3,2,1,0:T(8,128)(2,1)}, u32[]{:S(2)}) copy-start(bf16[1,2,256,256]{3,2,1,0:T(8,128)(2,1)} %get-tuple-element.92) | copy-start | bytes 786436
  152.8 12.9 %copy-start.23 = (bf16[1,2,256,256]{3,2,1,0:T(8,128)(2,1)S(1)}, bf16[1,2,256,256]{3,2,1,0:T(8,128)(2,1)}, u32[]{:S(2)}) copy-start(bf16[1,2,256,256]{3,2,1,0:T(8,128)(2,1)} %get-tuple-element.107) | copy-start | bytes 786436
  152.8 12.9 %copy-start.24 = (bf16[1,2,256,256]{3,2,1,0:T(8,128)(2,1)S(1)}, bf16[1,2,256,256]{3,2,1,0:T(8,128)(2,1)}, u32[]{:S(2)}) copy-start(bf16[1,2,256,256]{3,2,1,0:T(8,128)(2,1)} %get-tuple-element.101) | copy-start | bytes 786436
  152.8 12.9 %copy-start.25 = (bf16[1,2,256,256]{3,2,1,0:T(8,128)(2,1)S(1)}, bf16[1,2,256,256]{3,2,1,0:T(8,128)(2,1)}, u32[]{:S(2)}) copy-start(bf16[1,2,256,256]{3,2,1,0:T(8,128)(2,1)} %get-tuple-element.104) | copy-start | bytes 786436
  152.8 12.9 %copy-start.26 = (bf16[1,2,256,256]{3,2,1,0:T(8,128)(2,1)S(1)}, bf16[1,2,256,256]{3,2,1,0:T(8,128)(2,1)}, u32[]{:S(2)}) copy-start(bf16[1,2,256,256]{3,2,1,0:T(8,128)(2,1)} %get-tuple-element.98) | copy-start | bytes 786436
  167.1 25.7 %copy-start.8 = (f32[32,768]{0,1:T(8,128)S(1)}, f32[32,768]{0,1:T(8,128)}, u32[]{:S(2)}) copy-start(f32[32,768]{0,1:T(8,128)} %copy.20) | copy-start | bytes 294916
  167.1 25.7 %copy-start.9 = (f32[32,768]{0,1:T(8,128)S(1)}, f32[32,768]{0,1:T(8,128)}, u32[]{:S(2)}) copy-start(f32[32,768]{0,1:T(8,128)} %copy.21) | copy-start | bytes 294916
  167.1 26.9 %copy-start.7 = (bf16[768,64]{1,0:T(8,128)(2,1)S(1)}, bf16[768,64]{1,0:T(8,128)(2,1)}, u32[]{:S(2)}) copy-start(bf16[768,64]{1,0:T(8,128)(2,1)} %copy.17) | copy-start | bytes 294916
  189.2 51.4 %all-to-all-start.3 = ((bf16[4,4,256,256]{3,2,1,0:T(8,128)(2,1)}), bf16[4,4,256,256]{3,2,1,0:T(8,128)(2,1)S(1)}, u32[]{:S(2)}, u32[]{:S(2)}) async-start(bf16[4,4,256,256]{3,2,1,0:T(8,128)(2,1)} %maximum_maximum_fusion), calls=%async_computation.3 | async-start | bytes 4194304 | tf_op jit(solution)/shard_map/all_to_all | solution.py:422
  192.8 4.2 %copy-start.12 = (bf16[1,2,256,256]{3,2,1,0:T(8,128)(2,1)S(1)}, bf16[1,2,256,256]{3,2,1,0:T(8,128)(2,1)}, u32[]{:S(2)}) copy-start(bf16[1,2,256,256]{3,2,1,0:T(8,128)(2,1)} %get-tuple-element.109) | copy-start | bytes 786436
  192.8 4.2 %copy-start.13 = (bf16[1,2,256,256]{3,2,1,0:T(8,128)(2,1)S(1)}, bf16[1,2,256,256]{3,2,1,0:T(8,128)(2,1)}, u32[]{:S(2)}) copy-start(bf16[1,2,256,256]{3,2,1,0:T(8,128)(2,1)} %get-tuple-element.156) | copy-start | bytes 786436
  192.8 4.2 %copy-start.16 = (bf16[1,2,256,256]{3,2,1,0:T(8,128)(2,1)S(1)}, bf16[1,2,256,256]{3,2,1,0:T(8,128)(2,1)}, u32[]{:S(2)}) copy-start(bf16[1,2,256,256]{3,2,1,0:T(8,128)(2,1)} %get-tuple-element.94) | copy-start | bytes 786436
  192.8 4.2 %copy-start.17 = (bf16[1,2,256,256]{3,2,1,0:T(8,128)(2,1)S(1)}, bf16[1,2,256,256]{3,2,1,0:T(8,128)(2,1)}, u32[]{:S(2)}) copy-start(bf16[1,2,256,256]{3,2,1,0:T(8,128)(2,1)} %get-tuple-element.106) | copy-start | bytes 786436
  192.8 4.2 %copy-start.19 = (bf16[1,2,256,256]{3,2,1,0:T(8,128)(2,1)S(1)}, bf16[1,2,256,256]{3,2,1,0:T(8,128)(2,1)}, u32[]{:S(2)}) copy-start(bf16[1,2,256,256]{3,2,1,0:T(8,128)(2,1)} %get-tuple-element.100) | copy-start | bytes 786436
  241.9 52.2 %all-to-all-start.2 = ((bf16[4,4,256,256]{3,2,1,0:T(8,128)(2,1)}), bf16[4,4,256,256]{3,2,1,0:T(8,128)(2,1)}, u32[]{:S(2)}, u32[]{:S(2)}) async-start(bf16[4,4,256,256]{3,2,1,0:T(8,128)(2,1)} %maximum_maximum_fusion.1), calls=%async_computation.2 | async-start | bytes 4194304 | tf_op jit(solution)/shard_map/all_to_all | solution.py:422
  (21 other events, 51.6 us)
